TPU v7x, 512 devices: a whole 4x4x16 slice. The times are simulated.
512 devices in a mesh: tm: 128 (over z, y, core), mod: 4 (over x).
Axes of the slice: x: 4, y: 4, z: 16, core: 2. Of those that a mesh axis runs over, the one named last changes fastest.
Arguments:
- filterbank: bfloat16 [16384, 128], P('tm'), may hold values from -6 to 6
- conv_weight: bfloat16 [384, 1280], replicated, may hold values from -0.3125 to 0.3125
- mlp_gain: float32 [1280], replicated, may hold values from 0.25 to 1.75
- up_weight: bfloat16 [1280, 5120], P('tm', 'mod'), may hold values from -0.15625 to 0.15625
- down_weight: bfloat16 [5120, 1280], P('mod', 'tm'), may hold values from -0.078125 to 0.078125
- post_gain: float32 [1280], replicated, may hold values from 0.25 to 1.75
- audio_weight: bfloat16 [1280, 1792], P(None, 'mod'), may hold values from -0.15625 to 0.15625
- patches: bfloat16 [32768, 1280], P('tm'), may hold values from -6 to 6
- vision_gain: float32 [1280], replicated, may hold values from 0.25 to 1.75
- vision_weight: bfloat16 [5120, 1792], P('tm', 'mod'), may hold values from -0.078125 to 0.078125
- retention: int32 [128, 64], P('tm'), may hold values from 0 to 63, each once within a row
- kept_count: int32 [128], P('tm'), may hold values from 1 to 64, 4096 in all
Outputs:
- sequence: bfloat16 [128, 96, 1792], P('tm', None, 'mod')
Inputs may be any that keep to these rules, and one draw needn't show every extreme that they name: `retention`: each row lists every merged token of its frame once. `kept_count`: the counts sum to 4096.
All inputs are finite; a program needn't handle non-finite values. No bound on the sum of `kept_count` on one device may be relied on, other than what follows from the above.
Results may differ from a plain program's by a relative error of at most 0.01.
Values may be sent and summed in bfloat16 or wider, within the bound.
No kernel may reach another device: no remote copies, remote signals or barrier semaphores. Data moves between devices by JAX's collectives and lax.ppermute only.
A program may use at most 64 MiB of HBM per device.

v0:
```python
import jax
import jax.numpy as jnp
from jax import lax
from jax.experimental import pallas as pl
from jax.experimental.pallas import tpu as pltpu
from jax.sharding import Mesh, PartitionSpec as P


MRG_FRAME = 64
AUD_TOK = 64
SEQ_DEV = 96
D_ENC = 1280
D_LM = 448
Z = ("zh", "zl")
TM = Z + ("y", "c")
NZ, NY, NC, NM = 16, 4, 2, 4
WIDE = 3328
N_TM = NZ * NY * NC

BF = jnp.bfloat16
F32 = jnp.float32
NT = (((1,), (1,)), ((), ()))
VMEM = pl.BlockSpec(memory_space=pltpu.VMEM)


def arrival_spans():
    zl, c = lax.axis_index("zl"), lax.axis_index("c")
    block = jnp.arange(N_TM, dtype=jnp.int32)
    hop, zh, z_hop = block // NZ, (block // 4) % 4, block % 4
    shift = lambda k: jnp.where(k == 2, 3, jnp.where(k == 3, 2, k))
    from_z = 4 * zh + (zl + 4 - shift(z_hop)) % 4
    from_y = hop % NY
    from_c = jnp.where(hop < NY, c, 1 - c)
    return (8 * from_z + 2 * from_y + from_c).astype(jnp.int32)


def around(value, axis, size):
    shifts = (1, size - 1, 2)
    return [value] + [
        lax.ppermute(value, axis, [(i, (i + shift) % size) for i in range(size)])
        for shift in shifts
    ]


def swap_core(value):
    return lax.ppermute(value, "c", [(0, 1), (1, 0)])


def layer_norm(values, scale_gain):
    average = jnp.mean(values, axis=-1, keepdims=True)
    centred = values - average
    variance = jnp.mean(centred * centred, axis=-1, keepdims=True)
    return centred * lax.rsqrt(variance + 1e-05) * scale_gain


def rms_norm(values, scale_gain):
    square_mean = jnp.mean(values * values, axis=-1, keepdims=True)
    return values * lax.rsqrt(square_mean + 1e-06) * scale_gain


def dot(a, b):
    return jnp.dot(a, b, preferred_element_type=F32)


def erf_gelu(x):
    return 0.5 * x * (1.0 + lax.erf(x * 0.7071067811865476))


def pack_kernel(count_ref, up_ref, down_ref, vision_ref, out_ref):
    sides = (up_ref[8:].astype(F32), down_ref[8:].astype(F32))
    rest = [
        sides[row // 2][row % 2 : row % 2 + 1, 640 * half : 640 * half + 640]
        for half in range(2)
        for row in range(4)
    ]
    rest = jnp.concatenate(rest, axis=0).astype(BF)
    count = jnp.full((8, 128), count_ref[0].astype(F32), F32).astype(BF)
    blank = jnp.zeros((8, 64), BF)
    for peer in range(4):
        out_ref[peer, :, :1280] = up_ref[:8, :]
        out_ref[peer, :, 1280:2560] = down_ref[:8, :]
        out_ref[peer, :, 2560:3200] = rest
        out_ref[peer, :, 3200:WIDE] = count
        for k in range(5):
            start = WIDE + 512 * k
            rows = vision_ref[8 * k : 8 * k + 8, :]
            out_ref[peer, :, start : start + 512] = jnp.concatenate([rows, blank], axis=1)


def pack(kept_count, up_weight, down_rows, vision_weight):
    return pl.pallas_call(
        pack_kernel,
        out_shape=jax.ShapeDtypeStruct((4, 8, WIDE + 2560), BF),
        in_specs=[pl.BlockSpec(memory_space=pltpu.SMEM), VMEM, VMEM, VMEM],
        out_specs=VMEM,
        name="pack",
    )(kept_count, up_weight, down_rows, vision_weight)


def stem_kernel(
    frames_ref, before_ref, after_ref, conv_ref, gain_ref, order_ref, hidden_ref, pooled_ref, post_ref, rows
):
    frames = frames_ref[...].astype(F32)
    earlier = jnp.concatenate([before_ref[...].astype(F32), frames[:-1]], axis=0)
    later = jnp.concatenate([frames[1:], after_ref[...].astype(F32)], axis=0)
    unfolded = jnp.concatenate([earlier.astype(BF), frames_ref[...], later.astype(BF)], axis=1)
    gain = gain_ref[...]
    high = gain.astype(BF)
    middle = (gain - high.astype(F32)).astype(BF)
    low = (gain - high.astype(F32) - middle.astype(F32)).astype(BF)
    rows[:384, :] = conv_ref[...]
    rows[384:392, :] = high
    rows[392:400, :] = middle
    rows[400:408, :] = low
    rows[408:416, :] = jnp.zeros((8, D_ENC), BF)
    moved = jnp.zeros((416, D_ENC), F32)
    order = order_ref[...]
    for k in range(5):
        natural = lax.broadcasted_iota(jnp.int32, (256, D_ENC), 0) + 256 * k
        pick = jnp.where(natural == order, 1.0, 0.0).astype(BF)
        moved = moved + dot(rows[:, 256 * k : 256 * k + 256], pick)
    gains = moved[384:392] + moved[392:400] + moved[400:408]
    stem = erf_gelu(dot(unfolded, moved[:384].astype(BF))).astype(BF)
    hidden_ref[...] = layer_norm(stem.astype(F32), gains[0:1]).astype(BF)
    row = lax.broadcasted_iota(jnp.int32, (64, 128), 0)
    col = lax.broadcasted_iota(jnp.int32, (64, 128), 1)
    pair = jnp.where(col // 2 == row, 0.5, 0.0).astype(BF)
    pooled_ref[...] = dot(pair, stem)
    post_ref[...] = gains[1:2]


def make_stem(*args):
    return pl.pallas_call(
        stem_kernel,
        out_shape=(
            jax.ShapeDtypeStruct((128, D_ENC), BF),
            jax.ShapeDtypeStruct((64, D_ENC), F32),
            jax.ShapeDtypeStruct((1, D_ENC), F32),
        ),
        in_specs=[VMEM] * 6,
        out_specs=(VMEM,) * 3,
        scratch_shapes=[pltpu.VMEM((416, D_ENC), BF)],
        cost_estimate=pl.CostEstimate(
            flops=1_500_000_000, bytes_accessed=2_500_000, transcendentals=170_000
        ),
        name="stem",
    )(*args)


def ffn_kernel(hidden_ref, own_ref, other_ref, out_ref, count_ref, up, down, flat):
    for c, ref in enumerate((own_ref, other_ref)):
        rows = slice(512 * c, 512 * c + 512)
        up[rows, :] = ref[:, :1280]
        down[rows, :] = ref[:, 1280:2560]
        for tile in range(6):
            lanes = slice(2560 + 128 * tile, 2688 + 128 * tile)
            flat[tile, rows, :] = ref[:, lanes].astype(F32)
    for tile in range(5):
        for half in range(2):
            lanes = slice(640 * half + 128 * tile, 640 * half + 128 * tile + 128)
            for row in range(4):
                plane = flat[tile, pl.ds(half * 4 + row, N_TM, stride=8), :].astype(BF)
                into = up if row < 2 else down
                start = 1024 + (row % 2) * N_TM
                into[start : start + N_TM, lanes] = plane
    count_ref[...] = flat[5, pl.ds(0, N_TM, stride=8), :]
    row = lax.broadcasted_iota(jnp.int32, (64, 128), 0)
    col = lax.broadcasted_iota(jnp.int32, (64, 128), 1)
    pair = jnp.where(col // 2 == row, 0.5, 0.0).astype(BF)
    act = erf_gelu(dot(hidden_ref[...], up[...])).astype(BF)
    pooled = dot(pair, act).astype(BF)
    part = lax.dot_general(pooled, down[...], NT, preferred_element_type=F32).astype(BF)
    for peer in range(NM):
        out_ref[peer] = part


def ffn(hidden, own, other):
    return pl.pallas_call(
        ffn_kernel,
        out_shape=(
            jax.ShapeDtypeStruct((NM, 64, D_ENC), BF),
            jax.ShapeDtypeStruct((N_TM, 128), F32),
        ),
        in_specs=[VMEM] * 3,
        out_specs=(VMEM, VMEM),
        scratch_shapes=[
            pltpu.VMEM((1280, 1280), BF),
            pltpu.VMEM((1280, 1280), BF),
            pltpu.VMEM((6, 1024, 128), F32),
        ],
        cost_estimate=pl.CostEstimate(
            flops=650_000_000, bytes_accessed=8_000_000, transcendentals=170_000
        ),
        name="ffn",
    )(hidden, own, other)


def tail_kernel(
    place_ref, part_ref, stem_ref, gain_ref, audio_ref, vis_ref, rank_ref, count_ref, span_ref, out_ref
):
    me, kept = place_ref[0], place_ref[1]
    placed = count_ref[...] + float(AUD_TOK)
    slot = jnp.sum(jnp.where(span_ref[...] < me, placed, 0.0), axis=0, keepdims=True)
    row = lax.broadcasted_iota(jnp.int32, (N_TM, 128), 0)
    col = lax.broadcasted_iota(jnp.int32, (N_TM, 128), 1)
    local = (row - slot.astype(jnp.int32)) & (N_TM - 1)
    rank = jnp.where(col < 64, col, col - 64 + kept)
    take = (local == rank) & ((col >= 64) | (col < kept))
    take = jnp.where(take, 1.0, 0.0).astype(BF)
    total = stem_ref[...]
    for peer in range(NM):
        total = total + part_ref[peer].astype(F32)
    normed = layer_norm(total, gain_ref[...]).astype(BF)
    audio = dot(normed, audio_ref[...]).astype(BF)
    visual = vis_ref[0].astype(F32)
    for peer in range(1, 8):
        visual = visual + vis_ref[peer].astype(F32)
    visual = dot(rank_ref[...], visual.astype(BF)).astype(BF)
    picked = dot(take[:, :64], visual) + dot(take[:, 64:], audio)
    out_ref[...] = picked.astype(BF)


def tail(*args):
    return pl.pallas_call(
        tail_kernel,
        out_shape=jax.ShapeDtypeStruct((N_TM, D_LM), BF),
        in_specs=[pl.BlockSpec(memory_space=pltpu.SMEM)] + [VMEM] * 8,
        out_specs=VMEM,
        cost_estimate=pl.CostEstimate(
            flops=80_000_000, bytes_accessed=2_500_000, transcendentals=64
        ),
        name="tail",
    )(*args)


def merger_kernel(place_ref, *refs):
    blocks, tokens, out_ref, weight = refs[:4], refs[4:8], refs[8], refs[9]
    for hop in range(4):
        for zh in range(4):
            for k in range(5):
                start = zh * 160 + hop * 40 + k * 8
                weight[start : start + 8, :] = blocks[hop][zh, :, 512 * k : 512 * k + 512]
    for hop in range(4):
        for c in range(2):
            total = jnp.zeros((64, 512), F32)
            for zh in range(4):
                rows = tokens[hop][c, zh * 64 : zh * 64 + 64, :160]
                total = total + dot(rows, weight[zh * 160 : zh * 160 + 160, :])
            out_ref[place_ref[2 * hop + c]] = total[:, :D_LM].astype(BF)


def merger(place, blocks, tokens):
    return pl.pallas_call(
        merger_kernel,
        out_shape=jax.ShapeDtypeStruct((8, 64, D_LM), BF),
        in_specs=[pl.BlockSpec(memory_space=pltpu.SMEM)] + [VMEM] * 8,
        out_specs=VMEM,
        scratch_shapes=[pltpu.VMEM((640, 512), BF)],
        cost_estimate=pl.CostEstimate(
            flops=340_000_000, bytes_accessed=3_000_000, transcendentals=0
        ),
        name="merger",
    )(place, *blocks, *tokens)


def on_device(
    filterbank,
    conv_weight,
    mlp_gain,
    up_weight,
    down_weight,
    post_gain,
    audio_weight,
    patches,
    vision_gain,
    vision_weight,
    retention,
    kept_count,
):
    packed = pack(kept_count, up_weight, down_weight.T, vision_weight)
    packed, filterbank = lax.optimization_barrier((packed, filterbank))
    blocks = lax.all_to_all(packed, "zh", 0, 0)

    span = arrival_spans()
    main = (10 * span[:, None] + jnp.arange(8, dtype=jnp.int32)[None, :]).reshape(-1)
    rest = (10 * span[None, :] + 8 + jnp.arange(2, dtype=jnp.int32)[:, None]).reshape(-1)
    order = jnp.concatenate([main, rest])
    feature = lax.broadcasted_iota(jnp.int32, (D_ENC, D_ENC), 0)
    pick = (feature == order[None, :]).astype(BF)
    audio_rows = lax.dot_general(
        pick, audio_weight, (((0,), (0,)), ((), ())), preferred_element_type=F32
    ).astype(BF)
    up = [(i, i + 1) for i in range(N_TM - 1)]
    before = lax.ppermute(filterbank[-1:], TM, up)
    after = lax.ppermute(filterbank[:1], TM, [(j, i) for i, j in up])
    both_gains = jnp.pad(jnp.stack([mlp_gain, post_gain]), ((0, 6), (0, 0)))

    zl, y, c = lax.axis_index("zl"), lax.axis_index("y"), lax.axis_index("c")
    lane = jnp.arange(2048, dtype=jnp.int32)
    owner, inner = lane // 256, lane % 256
    shift = lambda k: jnp.where(k == 2, 3, jnp.where(k == 3, 2, k))
    owner_y = (y + NY - shift(owner % NY)) % NY
    owner_c = jnp.where(owner < NY, c, 1 - c)
    from_zl = (zl + 4 - shift(inner // 40)) % 4
    column = 40 * (8 * from_zl + 2 * owner_y + owner_c) + inner % 40
    column = jnp.where(inner < 160, column, -1)
    patch_feature = lax.broadcasted_iota(jnp.int32, (D_ENC, 2048), 0)
    pick_patch = (patch_feature == column[None, :]).astype(BF)
    patch_normed = rms_norm(patches.astype(F32), vision_gain).astype(BF)
    by_quarter = patch_normed.reshape(64, 4, D_ENC).transpose(1, 0, 2).reshape(256, D_ENC)
    slices = dot(by_quarter, pick_patch).astype(BF)
    core_slices = swap_core(slices[:, 1024:])
    ranks = jnp.arange(MRG_FRAME, dtype=jnp.int32)
    by_rank = (retention[0][:, None] == ranks[None, :]).astype(BF)

    ffn_hops = around(blocks[:, :, :WIDE], Z, NZ)
    tokens = []
    for hop, step in enumerate((0, 1, 3, 2)):
        lanes = slice(256 * hop, 256 * hop + 256)
        pair = jnp.stack([slices[:, lanes], core_slices[:, lanes]])
        back = [(i, (i - step) % NY) for i in range(NY)]
        tokens.append(pair if hop == 0 else lax.ppermute(pair, "y", back))
    ffn_z = jnp.concatenate(ffn_hops, axis=1)
    spread = jnp.broadcast_to(ffn_z[None], (NY,) + ffn_z.shape)
    own = lax.all_to_all(spread, "y", 0, 0).reshape(512, WIDE)
    hidden, pooled_stem, post = make_stem(
        filterbank, before, after, conv_weight, both_gains, order[None, :]
    )
    steps = jnp.asarray([0, 0, 1, 1, 3, 3, 2, 2], jnp.int32)
    flips = jnp.asarray([0, 1] * 4, jnp.int32)
    place = 2 * ((y + steps) % NY) + jnp.where(flips == 1, 1 - c, c)
    vis_hops = around(blocks[:, :, WIDE:], Z, NZ)
    partials = merger(place.astype(jnp.int32), vis_hops, tokens)
    partials = lax.all_to_all(partials, ("y", "c"), 0, 0)
    own, audio_rows, by_rank, hidden = lax.optimization_barrier(
        (own, audio_rows, by_rank, hidden)
    )
    other = swap_core(own)
    parts, counts = ffn(hidden, own, other)
    parts = lax.all_to_all(parts, "mod", 0, 0)
    me = lax.axis_index(TM).astype(jnp.int32)
    ids = jnp.arange(N_TM, dtype=jnp.int32)
    wide_span = jnp.broadcast_to(span[:, None], (N_TM, 128))
    ours = jnp.stack([me, kept_count[0]])
    send = tail(
        ours, parts, pooled_stem, post, audio_rows, partials, by_rank, counts, wide_span
    )
    counts, send = lax.optimization_barrier((counts, send))
    placed = counts[:, 0].astype(jnp.int32) + AUD_TOK
    began = jnp.sum(jnp.where(span[None, :] < ids[:, None], placed[None, :], 0), axis=1)
    length = jnp.sum(jnp.where(span[None, :] == ids[:, None], placed[None, :], 0), axis=1)
    moved = lax.all_to_all(send.reshape(N_TM, 1, D_LM), TM, 0, 0).reshape(N_TM, D_LM)

    offset = (me - began) % N_TM
    slot = jnp.where(offset < length, (began + offset) // N_TM, -1)
    slots = jnp.arange(SEQ_DEV, dtype=jnp.int32)
    put = (slot[None, :] == slots[:, None]).astype(BF)
    return dot(put, moved).astype(BF)[None]


def solution(mesh):
    split = Mesh(mesh.devices.reshape(4, 4, NY, NC, NM), TM + ("mod",))
    return jax.shard_map(
        on_device,
        mesh=split,
        in_specs=(
            P(TM, None),
            P(),
            P(),
            P(TM, "mod"),
            P("mod", TM),
            P(),
            P(None, "mod"),
            P(TM, None),
            P(),
            P(TM, "mod"),
            P(TM, None),
            P(TM),
        ),
        out_specs=P(TM, None, "mod"),
        check_vma=False,
    )
```

profile of v0, /device:TPU:1, one launch (start us, length us, event | category | flops | bytes accessed | tf_op | source)
XLA Modules:
  0.0 215.3 jit_solution(11520004060315974001)
XLA Ops:
  0.7 1.6 pack.1
  2.3 33.2 %all_to_all.25 = bf16[4,8,5888]{2,1,0:T(8,128)(2,1)S(1)} all-to-all(bf16[4,8,5888]{2,1,0:T(8,128)(2,1)} %pack.1), channel_id=1, replica_groups=mesh['zh'=4,'zl'=4,'y'=4,'c'=2,'mod'=4] {'zh'}, dimensions={0} | all-to-all | bytes 753664 | tf_op jit(solution)/shard_map/all_to_all | solution.py:282
  35.5 11.4 %collective-permute-start.2 = (bf16[4,8,3328]{2,1,0:T(8,128)(2,1)S(1)}, bf16[4,8,3328]{2,1,0:T(8,128)(2,1)S(1)}, u32[]{:S(2)}, u32[]{:S(2)}) collective-permute-start(bf16[4,8,3328]{2,1,0:T(8,128)(2,1)S(1)} %slice.56), channel_id=1, source_target_pairs={{0,64},{32,96},{64,128},{96,160},{128,192},{160,224},{192,256},{22... | collective-permute-start | bytes 638984 | tf_op jit(solution)/shard_map/ppermute | solution.py:40
  46.9 3.8 %collective-permute-start.1 = (bf16[4,8,3328]{2,1,0:T(8,128)(2,1)S(1)}, bf16[4,8,3328]{2,1,0:T(8,128)(2,1)S(1)}, u32[]{:S(2)}, u32[]{:S(2)}) collective-permute-start(bf16[4,8,3328]{2,1,0:T(8,128)(2,1)S(1)} %slice.56), channel_id=1, source_target_pairs={{0,480},{32,0},{64,32},{96,64},{128,96},{160,128},{192,160},{224,1... | collective-permute-start | bytes 638984 | tf_op jit(solution)/shard_map/ppermute | solution.py:40
  50.7 1.9 collective-permute-start
  52.6 4.0 %collective-permute-done.2 = bf16[4,8,3328]{2,1,0:T(8,128)(2,1)S(1)} collective-permute-done((bf16[4,8,3328]{2,1,0:T(8,128)(2,1)S(1)}, bf16[4,8,3328]{2,1,0:T(8,128)(2,1)S(1)}, u32[]{:S(2)}, u32[]{:S(2)}) %collective-permute-start.2) | collective-permute-done | bytes 213024 | tf_op jit(solution)/shard_map/ppermute | solution.py:40
  56.6 6.4 %collective-permute-done = bf16[4,8,3328]{2,1,0:T(8,128)(2,1)S(1)} collective-permute-done((bf16[4,8,3328]{2,1,0:T(8,128)(2,1)S(1)}, bf16[4,8,3328]{2,1,0:T(8,128)(2,1)S(1)}, u32[]{:S(2)}, u32[]{:S(2)}) %collective-permute-start) | collective-permute-done | bytes 213024 | tf_op jit(solution)/shard_map/ppermute | solution.py:40
  63.1 2.1 broadcast_in_dim.91
  65.2 4.8 %all-to-all-start.1 = ((bf16[4,4,32,3328]{3,2,1,0:T(8,128)(2,1)}), bf16[4,4,32,3328]{3,2,1,0:T(8,128)(2,1)}, u32[]{:S(2)}, u32[]{:S(2)}) async-start(bf16[4,4,32,3328]{3,2,1,0:T(8,128)(2,1)} %broadcast_in_dim.91), calls=%async_computation.1 | async-start | bytes 6815744 | tf_op jit(solution)/shard_map/all_to_all | solution.py:325
  70.0 0.7 fusion.58
  70.8 4.2 %collective-permute-start.3 = (bf16[1,128]{1,0:T(2,128)(2,1)S(1)}, bf16[1,128]{1,0:T(2,128)(2,1)S(1)}, u32[]{:S(2)}, u32[]{:S(2)}) collective-permute-start(bf16[1,128]{1,0:T(2,128)(2,1)S(1)} %get-tuple-element.44), channel_id=1, source_target_pairs={{0,4},{4,8},{8,12},{12,16},{16,20},{20,24},{24,28},{28,32},{32,36}... | collective-permute-start | bytes 776 | tf_op jit(solution)/shard_map/ppermute | solution.py:294
  74.9 1.9 collective-permute-start.4
  77.2 0.6 select_maximum_fusion.gain_ref
  77.8 3.0 %fusion.6.audio_ref = bf16[1280,448]{1,0:T(8,128)(2,1)} fusion(bf16[1280,448]{0,1:T(8,128)(2,1)S(1)} %copy-done, s32[1280]{0:T(1024)S(1)} %pad_add_fusion), kind=kOutput, calls=%fused_computation.7 | convolution fusion | flops 1471856640 | bytes 2298880 | tf_op jit(solution)/shard_map/dot_general | solution.py:290
  80.8 0.7 fusion.15.rank_ref
  81.5 0.6 broadcast_in_dim.92.order_ref
  82.1 24.4 %collective-permute-done.3.before_ref = bf16[1,128]{1,0:T(2,128)(2,1)S(1)} collective-permute-done((bf16[1,128]{1,0:T(2,128)(2,1)S(1)}, bf16[1,128]{1,0:T(2,128)(2,1)S(1)}, u32[]{:S(2)}, u32[]{:S(2)}) %collective-permute-start.3) | collective-permute-done | bytes 288 | tf_op jit(solution)/shard_map/ppermute | solution.py:294
  106.5 3.0 %collective-permute-done.4.after_ref = bf16[1,128]{1,0:T(2,128)(2,1)S(1)} collective-permute-done((bf16[1,128]{1,0:T(2,128)(2,1)S(1)}, bf16[1,128]{1,0:T(2,128)(2,1)S(1)}, u32[]{:S(2)}, u32[]{:S(2)}) %collective-permute-start.4) | collective-permute-done | bytes 288 | tf_op jit(solution)/shard_map/ppermute | solution.py:295
  109.5 0.6 copy-done.19
  110.1 4.2 %stem.1 = (bf16[128,1280]{1,0:T(8,128)(2,1)}, f32[64,1280]{1,0:T(8,128)}, f32[1,1280]{1,0:T(1,128)}) custom-call(bf16[128,128]{1,0:T(8,128)(2,1)} %frames_ref, bf16[1,128]{1,0:T(2,128)(2,1)} %copy-done.18, bf16[1,128]{1,0:T(2,128)(2,1)} %copy-done.19, bf16[384,1280]{1,0:T(8,128)(2,1)} %conv_ref.1, f32[8,1280]{1,0:T(8,128)} %select_maximum_fusion.gain_ref, ...), custom_call_target="tpu_custom_call" | custom-call | flops 1500000000 | bytes 2500000 | tf_op jit(solution)/shard_map/stem/pallas_call | solution.py:133
  114.3 1.9 collective-permute-start.5
  117.0 2.2 %fusion.9 = bf16[256,2048]{1,0:T(8,128)(2,1)S(1)} fusion(bf16[256,1280]{1,0:T(8,128)(2,1)S(1)} %bitcast.33, s32[2048]{0:T(1024)S(1)} %fusion.23), kind=kOutput, calls=%fused_computation.8 | convolution fusion | flops 1345323008 | bytes 1712128 | tf_op jit(solution)/shard_map/dot_general | solution.py:62
  119.3 2.4 %collective-permute-start.9 = (bf16[256,1024]{1,0:T(8,128)(2,1)S(1)}, bf16[256,1024]{1,0:T(8,128)(2,1)S(1)}, u32[]{:S(2)}, u32[]{:S(2)}) collective-permute-start(bf16[256,1024]{1,0:T(8,128)(2,1)S(1)} %slice.59), channel_id=1, source_target_pairs={{0,4},{4,0},{1,5},{5,1},{2,6},{6,2},{3,7},{7,3},{8,12},{12,8},{9,1... | collective-permute-start | bytes 1572872 | tf_op jit(solution)/shard_map/ppermute | solution.py:46
  121.8 1.4 collective-permute-done.9
  123.3 3.2 %collective-permute-start.10 = (bf16[2,256,256]{2,1,0:T(8,128)(2,1)S(1)}, bf16[2,256,256]{2,1,0:T(8,128)(2,1)S(1)}, u32[]{:S(2)}, u32[]{:S(2)}) collective-permute-start(bf16[2,256,256]{2,1,0:T(8,128)(2,1)S(1)} %pad_maximum_fusion.2), channel_id=1, source_target_pairs={{0,24},{8,0},{16,8},{24,16},{1,25},{9,1},{17,9},{25,17},{2,26},{10... | collective-permute-start | bytes 786440 | tf_op jit(solution)/shard_map/ppermute | solution.py:322
  126.6 2.0 collective-permute-start.11
  128.7 4.0 %collective-permute-start.12 = (bf16[2,256,256]{2,1,0:T(8,128)(2,1)S(1)}, bf16[2,256,256]{2,1,0:T(8,128)(2,1)S(1)}, u32[]{:S(2)}, u32[]{:S(2)}) collective-permute-start(bf16[2,256,256]{2,1,0:T(8,128)(2,1)S(1)} %pad_maximum_fusion.4), channel_id=1, source_target_pairs={{0,16},{8,24},{16,0},{24,8},{1,17},{9,25},{17,1},{25,9},{2,18},{10... | collective-permute-start | bytes 786440 | tf_op jit(solution)/shard_map/ppermute | solution.py:322
  132.7 1.9 collective-permute-start.6
  134.7 4.6 %collective-permute-start.7 = (bf16[4,8,2560]{2,1,0:T(8,128)(2,1)S(1)}, bf16[4,8,2560]{2,1,0:T(8,128)(2,1)S(1)}, u32[]{:S(2)}, u32[]{:S(2)}) collective-permute-start(bf16[4,8,2560]{2,1,0:T(8,128)(2,1)S(1)} %slice.57.refs_0_), channel_id=1, source_target_pairs={{0,480},{32,0},{64,32},{96,64},{128,96},{160,128},{192,160},{224,1... | collective-permute-start | bytes 491528 | tf_op jit(solution)/shard_map/ppermute | solution.py:40
  139.3 1.9 collective-permute-start.8
  141.7 0.7 pad_maximum_fusion.1.refs_4_
  142.5 6.2 %collective-permute-done.8.refs_3_ = bf16[4,8,2560]{2,1,0:T(8,128)(2,1)S(1)} collective-permute-done((bf16[4,8,2560]{2,1,0:T(8,128)(2,1)S(1)}, bf16[4,8,2560]{2,1,0:T(8,128)(2,1)S(1)}, u32[]{:S(2)}, u32[]{:S(2)}) %collective-permute-start.8) | collective-permute-done | bytes 163872 | tf_op jit(solution)/shard_map/ppermute | solution.py:40
  148.7 0.6 copy-done.11
  149.4 3.1 %merger.1 = bf16[8,64,448]{2,1,0:T(8,128)(2,1)} custom-call(s32[8]{0:T(128)} %fusion.46.place_ref, bf16[4,8,2560]{2,1,0:T(8,128)(2,1)} %copy-done.4, bf16[4,8,2560]{2,1,0:T(8,128)(2,1)} %copy-done.9, bf16[4,8,2560]{2,1,0:T(8,128)(2,1)} %copy-done.10, bf16[4,8,2560]{2,1,0:T(8,128)(2,1)} %copy-done.11, bf16[2,256,256]{2,1,0:T(8,128)(2,1)} %pad_maximum_fusion.1.refs_4_, ...), custom_call_target="tpu_custom_call" | custom-call | flops 340000000 | bytes 3000000 | tf_op jit(solution)/shard_map/merger/pallas_call | solution.py:253
  152.5 8.1 %all-to-all-start.3 = ((bf16[8,64,448]{2,1,0:T(8,128)(2,1)}), bf16[8,64,448]{2,1,0:T(8,128)(2,1)S(1)}, u32[]{:S(2)}, u32[]{:S(2)}) async-start(bf16[8,64,448]{2,1,0:T(8,128)(2,1)} %merger.1), calls=%async_computation.3 | async-start | bytes 1048576 | tf_op jit(solution)/shard_map/all_to_all | solution.py:334
  160.6 6.0 %ffn.1 = (bf16[4,64,1280]{2,1,0:T(8,128)(2,1)}, f32[128,128]{1,0:T(8,128)}) custom-call(bf16[128,1280]{1,0:T(8,128)(2,1)} %get-tuple-element.21.hidden_ref, bf16[512,3328]{1,0:T(8,128)(2,1)} %bitcast.1.own_ref, bf16[512,3328]{1,0:T(8,128)(2,1)} %collective-permute-done.5.other_ref), custom_call_target="tpu_custom_call" | custom-call | flops 650000000 | bytes 8000000 | tf_op jit(solution)/shard_map/ffn/pallas_call | solution.py:178
  166.6 3.3 %all-to-all-done.3.vis_ref = bf16[8,64,448]{2,1,0:T(8,128)(2,1)S(1)} async-done(((bf16[8,64,448]{2,1,0:T(8,128)(2,1)}), bf16[8,64,448]{2,1,0:T(8,128)(2,1)S(1)}, u32[]{:S(2)}, u32[]{:S(2)}) %all-to-all-start.3) | async-done | bytes 458784 | tf_op jit(solution)/shard_map/all_to_all | solution.py:334
  169.9 4.0 %all-to-all-start.2 = ((bf16[4,64,1280]{2,1,0:T(8,128)(2,1)}), bf16[4,64,1280]{2,1,0:T(8,128)(2,1)S(1)}, u32[]{:S(2)}, u32[]{:S(2)}) async-start(bf16[4,64,1280]{2,1,0:T(8,128)(2,1)} %get-tuple-element.24), calls=%async_computation.2 | async-start | bytes 1310720 | tf_op jit(solution)/shard_map/all_to_all | solution.py:340
  174.0 0.6 pad_add_fusion.1.place_ref
  174.5 9.2 %all-to-all-done.2.part_ref = bf16[4,64,1280]{2,1,0:T(8,128)(2,1)S(1)} async-done(((bf16[4,64,1280]{2,1,0:T(8,128)(2,1)}), bf16[4,64,1280]{2,1,0:T(8,128)(2,1)S(1)}, u32[]{:S(2)}, u32[]{:S(2)}) %all-to-all-start.2) | async-done | bytes 655392 | tf_op jit(solution)/shard_map/all_to_all | solution.py:340
  183.7 0.8 broadcast_in_dim.98.span_ref
  184.6 3.2 %tail.1 = bf16[128,448]{1,0:T(8,128)(2,1)} custom-call(s32[2]{0:T(128)} %pad_add_fusion.1.place_ref, bf16[4,64,1280]{2,1,0:T(8,128)(2,1)} %copy-done.2, f32[64,1280]{1,0:T(8,128)} %get-tuple-element.25.stem_ref, f32[1,1280]{1,0:T(1,128)} %get-tuple-element.26.gain_ref, bf16[1280,448]{1,0:T(8,128)(2,1)} %fusion.6.audio_ref, bf16[8,64,448]{2,1,0:T(8,128)(2,1)} %copy-done.3, ...), custom_call_target="tpu_custom_call" | custom-call | flops 80000000 | bytes 2500000 | tf_op jit(solution)/shard_map/tail/pallas_call | solution.py:224
  187.8 0.6 broadcast.966
  188.3 1.6 reduce.2
  189.9 0.8 reshape.327
  190.7 7.3 %all-to-all-start.4 = ((bf16[128,2,224]{2,1,0:T(2,128)(2,1)}), bf16[128,2,224]{2,1,0:T(2,128)(2,1)S(1)}, u32[]{:S(2)}, u32[]{:S(2)}) async-start(bf16[128,2,224]{2,1,0:T(2,128)(2,1)} %reshape.327), calls=%async_computation.4 | async-start | bytes 262144 | tf_op jit(solution)/shard_map/all_to_all | solution.py:352
  198.2 15.8 %all-to-all-done.4 = bf16[128,2,224]{2,1,0:T(2,128)(2,1)S(1)} async-done(((bf16[128,2,224]{2,1,0:T(2,128)(2,1)}), bf16[128,2,224]{2,1,0:T(2,128)(2,1)S(1)}, u32[]{:S(2)}, u32[]{:S(2)}) %all-to-all-start.4) | async-done | bytes 114720 | tf_op jit(solution)/shard_map/all_to_all | solution.py:352
  214.4 0.8 fusion.13
  (75 shorter events, 2.4 us)
Async XLA Ops:
  0.0 77.8 %copy-start = (bf16[1280,448]{0,1:T(8,128)(2,1)S(1)}, bf16[1280,448]{0,1:T(8,128)(2,1)}, u32[]{:S(2)}) copy-start(bf16[1280,448]{0,1:T(8,128)(2,1)} %param.20) | copy-start | bytes 3440644
  35.5 21.1 %collective-permute-start.2 = (bf16[4,8,3328]{2,1,0:T(8,128)(2,1)S(1)}, bf16[4,8,3328]{2,1,0:T(8,128)(2,1)S(1)}, u32[]{:S(2)}, u32[]{:S(2)}) collective-permute-start(bf16[4,8,3328]{2,1,0:T(8,128)(2,1)S(1)} %slice.56), channel_id=1, source_target_pairs={{0,64},{32,96},{64,128},{96,160},{128,192},{160,224},{192,256},{22... | collective-permute-start | bytes 638984 | tf_op jit(solution)/shard_map/ppermute | solution.py:40
  46.9 9.7 %collective-permute-start.1 = (bf16[4,8,3328]{2,1,0:T(8,128)(2,1)S(1)}, bf16[4,8,3328]{2,1,0:T(8,128)(2,1)S(1)}, u32[]{:S(2)}, u32[]{:S(2)}) collective-permute-start(bf16[4,8,3328]{2,1,0:T(8,128)(2,1)S(1)} %slice.56), channel_id=1, source_target_pairs={{0,480},{32,0},{64,32},{96,64},{128,96},{160,128},{192,160},{224,1... | collective-permute-start | bytes 638984 | tf_op jit(solution)/shard_map/ppermute | solution.py:40
  50.7 12.3 %collective-permute-start = (bf16[4,8,3328]{2,1,0:T(8,128)(2,1)S(1)}, bf16[4,8,3328]{2,1,0:T(8,128)(2,1)S(1)}, u32[]{:S(2)}, u32[]{:S(2)}) collective-permute-start(bf16[4,8,3328]{2,1,0:T(8,128)(2,1)S(1)} %slice.56), channel_id=1, source_target_pairs={{0,32},{32,64},{64,96},{96,128},{128,160},{160,192},{192,224},{224... | collective-permute-start | bytes 638984 | tf_op jit(solution)/shard_map/ppermute | solution.py:40
  65.2 11.9 %copy-start.13 = (f32[1280]{0:T(1024)S(1)}, f32[1280]{0:T(1024)}, u32[]{:S(2)}) copy-start(f32[1280]{0:T(1024)} %param.19) | copy-start | bytes 15364
  65.2 11.9 %copy-start.14 = (f32[1280]{0:T(1024)S(1)}, f32[1280]{0:T(1024)}, u32[]{:S(2)}) copy-start(f32[1280]{0:T(1024)} %param.16) | copy-start | bytes 15364
  65.2 49.1 %all-to-all-start.1 = ((bf16[4,4,32,3328]{3,2,1,0:T(8,128)(2,1)}), bf16[4,4,32,3328]{3,2,1,0:T(8,128)(2,1)}, u32[]{:S(2)}, u32[]{:S(2)}) async-start(bf16[4,4,32,3328]{3,2,1,0:T(8,128)(2,1)} %broadcast_in_dim.91), calls=%async_computation.1 | async-start | bytes 6815744 | tf_op jit(solution)/shard_map/all_to_all | solution.py:325
  70.8 35.8 %collective-permute-start.3 = (bf16[1,128]{1,0:T(2,128)(2,1)S(1)}, bf16[1,128]{1,0:T(2,128)(2,1)S(1)}, u32[]{:S(2)}, u32[]{:S(2)}) collective-permute-start(bf16[1,128]{1,0:T(2,128)(2,1)S(1)} %get-tuple-element.44), channel_id=1, source_target_pairs={{0,4},{4,8},{8,12},{12,16},{16,20},{20,24},{24,28},{28,32},{32,36}... | collective-permute-start | bytes 776 | tf_op jit(solution)/shard_map/ppermute | solution.py:294
  74.9 34.6 %collective-permute-start.4 = (bf16[1,128]{1,0:T(2,128)(2,1)S(1)}, bf16[1,128]{1,0:T(2,128)(2,1)S(1)}, u32[]{:S(2)}, u32[]{:S(2)}) collective-permute-start(bf16[1,128]{1,0:T(2,128)(2,1)S(1)} %get-tuple-element.43), channel_id=1, source_target_pairs={{4,0},{8,4},{12,8},{16,12},{20,16},{24,20},{28,24},{32,28},{36,32}... | collective-permute-start | bytes 776 | tf_op jit(solution)/shard_map/ppermute | solution.py:295
  77.8 3.0 %copy-start.15 = (s32[1,64]{1,0:T(1,128)S(1)}, s32[1,64]{1,0:T(1,128)}, u32[]{:S(2)}) copy-start(s32[1,64]{1,0:T(1,128)} %param.24) | copy-start | bytes 772
  82.1 34.2 %copy-start.1 = (bf16[256,1280]{1,0:T(8,128)(2,1)S(1)}, bf16[256,1280]{1,0:T(8,128)(2,1)}, u32[]{:S(2)}) copy-start(bf16[256,1280]{1,0:T(8,128)(2,1)} %param.21) | copy-start | bytes 1966084
  82.1 34.4 %copy-start.12 = (f32[1280]{0:T(1024)S(1)}, f32[1280]{0:T(1024)}, u32[]{:S(2)}) copy-start(f32[1280]{0:T(1024)} %param.22) | copy-start | bytes 15364
  106.5 3.0 %copy-start.18 = (bf16[1,128]{1,0:T(2,128)(2,1)}, bf16[1,128]{1,0:T(2,128)(2,1)S(1)}, u32[]{:S(2)}) copy-start(bf16[1,128]{1,0:T(2,128)(2,1)S(1)} %collective-permute-done.3.before_ref) | copy-start | bytes 772
  109.5 0.6 copy-start.19
  114.3 46.2 %collective-permute-start.5 = (bf16[512,3328]{1,0:T(8,128)(2,1)}, bf16[512,3328]{1,0:T(8,128)(2,1)}, u32[]{:S(2)}, u32[]{:S(2)}) collective-permute-start(bf16[512,3328]{1,0:T(8,128)(2,1)} %bitcast.1.own_ref), channel_id=1, source_target_pairs={{0,4},{4,0},{1,5},{5,1},{2,6},{6,2},{3,7},{7,3},{8,12},{12,8},{9,1... | collective-permute-start | bytes 10223624 | tf_op jit(solution)/shard_map/ppermute | solution.py:46
  119.3 3.9 %collective-permute-start.9 = (bf16[256,1024]{1,0:T(8,128)(2,1)S(1)}, bf16[256,1024]{1,0:T(8,128)(2,1)S(1)}, u32[]{:S(2)}, u32[]{:S(2)}) collective-permute-start(bf16[256,1024]{1,0:T(8,128)(2,1)S(1)} %slice.59), channel_id=1, source_target_pairs={{0,4},{4,0},{1,5},{5,1},{2,6},{6,2},{3,7},{7,3},{8,12},{12,8},{9,1... | collective-permute-start | bytes 1572872 | tf_op jit(solution)/shard_map/ppermute | solution.py:46
  121.8 19.4 %copy-start.16 = (s32[8]{0:T(128)S(1)}, s32[8]{0:T(128)}, u32[]{:S(2)}) copy-start(s32[8]{0:T(128)} %constant.219.clone) | copy-start | bytes 100
  121.8 19.4 %copy-start.17 = (pred[8]{0:T(512)(128)(4,1)S(1)}, pred[8]{0:T(512)(128)(4,1)}, u32[]{:S(2)}) copy-start(pred[8]{0:T(512)(128)(4,1)} %constant.228) | copy-start | bytes 28
  123.3 11.3 %collective-permute-start.10 = (bf16[2,256,256]{2,1,0:T(8,128)(2,1)S(1)}, bf16[2,256,256]{2,1,0:T(8,128)(2,1)S(1)}, u32[]{:S(2)}, u32[]{:S(2)}) collective-permute-start(bf16[2,256,256]{2,1,0:T(8,128)(2,1)S(1)} %pad_maximum_fusion.2), channel_id=1, source_target_pairs={{0,24},{8,0},{16,8},{24,16},{1,25},{9,1},{17,9},{25,17},{2,26},{10... | collective-permute-start | bytes 786440 | tf_op jit(solution)/shard_map/ppermute | solution.py:322
  126.6 12.6 %collective-permute-start.11 = (bf16[2,256,256]{2,1,0:T(8,128)(2,1)S(1)}, bf16[2,256,256]{2,1,0:T(8,128)(2,1)S(1)}, u32[]{:S(2)}, u32[]{:S(2)}) collective-permute-start(bf16[2,256,256]{2,1,0:T(8,128)(2,1)S(1)} %pad_maximum_fusion.3), channel_id=1, source_target_pairs={{0,8},{8,16},{16,24},{24,0},{1,9},{9,17},{17,25},{25,1},{2,10},{10... | collective-permute-start | bytes 786440 | tf_op jit(solution)/shard_map/ppermute | solution.py:322
  128.7 13.8 %collective-permute-start.12 = (bf16[2,256,256]{2,1,0:T(8,128)(2,1)S(1)}, bf16[2,256,256]{2,1,0:T(8,128)(2,1)S(1)}, u32[]{:S(2)}, u32[]{:S(2)}) collective-permute-start(bf16[2,256,256]{2,1,0:T(8,128)(2,1)S(1)} %pad_maximum_fusion.4), channel_id=1, source_target_pairs={{0,16},{8,24},{16,0},{24,8},{1,17},{9,25},{17,1},{25,9},{2,18},{10... | collective-permute-start | bytes 786440 | tf_op jit(solution)/shard_map/ppermute | solution.py:322
  132.7 16.0 %copy-start.4 = (bf16[4,8,2560]{2,1,0:T(8,128)(2,1)}, bf16[4,8,2560]{2,1,0:T(8,128)(2,1)S(1)}, u32[]{:S(2)}) copy-start(bf16[4,8,2560]{2,1,0:T(8,128)(2,1)S(1)} %slice.57.refs_0_) | copy-start | bytes 491524
  132.7 9.8 %collective-permute-start.6 = (bf16[4,8,2560]{2,1,0:T(8,128)(2,1)S(1)}, bf16[4,8,2560]{2,1,0:T(8,128)(2,1)S(1)}, u32[]{:S(2)}, u32[]{:S(2)}) collective-permute-start(bf16[4,8,2560]{2,1,0:T(8,128)(2,1)S(1)} %slice.57.refs_0_), channel_id=1, source_target_pairs={{0,32},{32,64},{64,96},{96,128},{128,160},{160,192},{192,224},{224... | collective-permute-start | bytes 491528 | tf_op jit(solution)/shard_map/ppermute | solution.py:40
  134.7 14.0 %copy-start.5 = (bf16[2,256,256]{2,1,0:T(8,128)(2,1)}, bf16[2,256,256]{2,1,0:T(8,128)(2,1)S(1)}, u32[]{:S(2)}) copy-start(bf16[2,256,256]{2,1,0:T(8,128)(2,1)S(1)} %collective-permute-done.10.refs_5_) | copy-start | bytes 786436
  134.7 7.8 %collective-permute-start.7 = (bf16[4,8,2560]{2,1,0:T(8,128)(2,1)S(1)}, bf16[4,8,2560]{2,1,0:T(8,128)(2,1)S(1)}, u32[]{:S(2)}, u32[]{:S(2)}) collective-permute-start(bf16[4,8,2560]{2,1,0:T(8,128)(2,1)S(1)} %slice.57.refs_0_), channel_id=1, source_target_pairs={{0,480},{32,0},{64,32},{96,64},{128,96},{160,128},{192,160},{224,1... | collective-permute-start | bytes 491528 | tf_op jit(solution)/shard_map/ppermute | solution.py:40
  139.3 9.4 %copy-start.6 = (bf16[2,256,256]{2,1,0:T(8,128)(2,1)}, bf16[2,256,256]{2,1,0:T(8,128)(2,1)S(1)}, u32[]{:S(2)}) copy-start(bf16[2,256,256]{2,1,0:T(8,128)(2,1)S(1)} %collective-permute-done.11.refs_6_) | copy-start | bytes 786436
  139.3 9.4 %collective-permute-start.8 = (bf16[4,8,2560]{2,1,0:T(8,128)(2,1)S(1)}, bf16[4,8,2560]{2,1,0:T(8,128)(2,1)S(1)}, u32[]{:S(2)}, u32[]{:S(2)}) collective-permute-start(bf16[4,8,2560]{2,1,0:T(8,128)(2,1)S(1)} %slice.57.refs_0_), channel_id=1, source_target_pairs={{0,64},{32,96},{64,128},{96,160},{128,192},{160,224},{192,256},{22... | collective-permute-start | bytes 491528 | tf_op jit(solution)/shard_map/ppermute | solution.py:40
  142.5 6.2 %copy-start.7 = (bf16[2,256,256]{2,1,0:T(8,128)(2,1)}, bf16[2,256,256]{2,1,0:T(8,128)(2,1)S(1)}, u32[]{:S(2)}) copy-start(bf16[2,256,256]{2,1,0:T(8,128)(2,1)S(1)} %collective-permute-done.12.refs_7_) | copy-start | bytes 786436
  142.5 6.2 %copy-start.9 = (bf16[4,8,2560]{2,1,0:T(8,128)(2,1)}, bf16[4,8,2560]{2,1,0:T(8,128)(2,1)S(1)}, u32[]{:S(2)}) copy-start(bf16[4,8,2560]{2,1,0:T(8,128)(2,1)S(1)} %collective-permute-done.6.refs_1_) | copy-start | bytes 491524
  142.5 6.2 %copy-start.10 = (bf16[4,8,2560]{2,1,0:T(8,128)(2,1)}, bf16[4,8,2560]{2,1,0:T(8,128)(2,1)S(1)}, u32[]{:S(2)}) copy-start(bf16[4,8,2560]{2,1,0:T(8,128)(2,1)S(1)} %collective-permute-done.7.refs_2_) | copy-start | bytes 491524
  148.7 0.7 copy-start.11
  152.5 17.4 %all-to-all-start.3 = ((bf16[8,64,448]{2,1,0:T(8,128)(2,1)}), bf16[8,64,448]{2,1,0:T(8,128)(2,1)S(1)}, u32[]{:S(2)}, u32[]{:S(2)}) async-start(bf16[8,64,448]{2,1,0:T(8,128)(2,1)} %merger.1), calls=%async_computation.3 | async-start | bytes 1048576 | tf_op jit(solution)/shard_map/all_to_all | solution.py:334
  169.9 14.6 %copy-start.3 = (bf16[8,64,448]{2,1,0:T(8,128)(2,1)}, bf16[8,64,448]{2,1,0:T(8,128)(2,1)S(1)}, u32[]{:S(2)}) copy-start(bf16[8,64,448]{2,1,0:T(8,128)(2,1)S(1)} %all-to-all-done.3.vis_ref) | copy-start | bytes 1376260
  169.9 13.7 %all-to-all-start.2 = ((bf16[4,64,1280]{2,1,0:T(8,128)(2,1)}), bf16[4,64,1280]{2,1,0:T(8,128)(2,1)S(1)}, u32[]{:S(2)}, u32[]{:S(2)}) async-start(bf16[4,64,1280]{2,1,0:T(8,128)(2,1)} %get-tuple-element.24), calls=%async_computation.2 | async-start | bytes 1310720 | tf_op jit(solution)/shard_map/all_to_all | solution.py:340
  183.7 0.9 copy-start.2
  184.5 13.4 %copy-start.8 = (f32[128,128]{1,0:T(8,128)S(1)}, f32[128,128]{1,0:T(8,128)}, u32[]{:S(2)}) copy-start(f32[128,128]{1,0:T(8,128)} %get-tuple-element.29.count_ref) | copy-start | bytes 196612
  190.7 23.4 %all-to-all-start.4 = ((bf16[128,2,224]{2,1,0:T(2,128)(2,1)}), bf16[128,2,224]{2,1,0:T(2,128)(2,1)S(1)}, u32[]{:S(2)}, u32[]{:S(2)}) async-start(bf16[128,2,224]{2,1,0:T(2,128)(2,1)} %reshape.327), calls=%async_computation.4 | async-start | bytes 262144 | tf_op jit(solution)/shard_map/all_to_all | solution.py:352
where the time goes:
time: 216 us; the launch traced here: 215 us
  waiting for transfers between devices  73.8 us (34%)
  starting transfers between devices  69.4 us (32%)
  blocking collectives  33.2 us (15%)
  Pallas kernels  18.1 us (8%)
  local copies, waits for them, and re-layouts  7.74 us (4%)
  matrix products  6.09 us (3%)
  other arithmetic  5.66 us (3%)
    all_to_all x1, blocking collectives, on_device(): blocks = lax.all_to_all(packed, 'zh', 0, 0)  33.2 us
    ppermute x6, starting transfers between devices, around(): lax.ppermute(value, axis, [(i, (i + shift) % size) for i in range(size)])  25.5 us
    ppermute x1, waiting for transfers between devices, on_device(): before = lax.ppermute(filterbank[-1:], TM, up)  24.4 us
    ppermute x6, waiting for transfers between devices, around(): lax.ppermute(value, axis, [(i, (i + shift) % size) for i in range(size)])  16.6 us
    all_to_all x1, waiting for transfers between devices, on_device(): lax.all_to_all(send.reshape(N_TM, 1, D_LM), TM, 0, 0).reshape(N_TM, D_LM)  15.8 us
    ppermute x3, starting transfers between devices, on_device(): tokens.append(pair if hop == 0 else lax.ppermute(pair, 'y', back))  9.28 us
    all_to_all x1, waiting for transfers between devices, on_device(): parts = lax.all_to_all(parts, 'mod', 0, 0)  9.16 us
    all_to_all x1, starting transfers between devices, on_device(): partials = lax.all_to_all(partials, ('y', 'c'), 0, 0)  8.07 us
  transfers between devices with their start and end apart: 17, of which 9 were waited for; matrix products, arithmetic and copies ran while one was open for 5% of the time, Pallas kernels for 6%

commit v1 on v0

--- a/solution.py
+++ b/solution.py
@@ -6,7 +6,6 @@
 from jax.sharding import Mesh, PartitionSpec as P
 
 
-MRG_FRAME = 64
 AUD_TOK = 64
 SEQ_DEV = 96
 D_ENC = 1280
@@ -20,6 +19,7 @@
 BF = jnp.bfloat16
 F32 = jnp.float32
 NT = (((1,), (1,)), ((), ()))
+TN = (((0,), (0,)), ((), ()))
 VMEM = pl.BlockSpec(memory_space=pltpu.VMEM)
 
 
@@ -143,6 +143,7 @@
         cost_estimate=pl.CostEstimate(
             flops=1_500_000_000, bytes_accessed=2_500_000, transcendentals=170_000
         ),
+        compiler_params=pltpu.CompilerParams(vmem_limit_bytes=16 << 20),
         name="stem",
     )(*args)
 
@@ -191,6 +192,7 @@
         cost_estimate=pl.CostEstimate(
             flops=650_000_000, bytes_accessed=8_000_000, transcendentals=170_000
         ),
+        compiler_params=pltpu.CompilerParams(vmem_limit_bytes=32 << 20),
         name="ffn",
     )(hidden, own, other)
 
@@ -215,7 +217,9 @@
     visual = vis_ref[0].astype(F32)
     for peer in range(1, 8):
         visual = visual + vis_ref[peer].astype(F32)
-    visual = dot(rank_ref[...], visual.astype(BF)).astype(BF)
+    token = lax.broadcasted_iota(jnp.int32, (64, 64), 0)
+    by_rank = jnp.where(token == rank_ref[...], 1.0, 0.0).astype(BF)
+    visual = lax.dot_general(by_rank, visual.astype(BF), TN, preferred_element_type=F32).astype(BF)
     picked = dot(take[:, :64], visual) + dot(take[:, 64:], audio)
     out_ref[...] = picked.astype(BF)
 
@@ -229,12 +233,13 @@
         cost_estimate=pl.CostEstimate(
             flops=80_000_000, bytes_accessed=2_500_000, transcendentals=64
         ),
+        compiler_params=pltpu.CompilerParams(vmem_limit_bytes=12 << 20),
         name="tail",
     )(*args)
 
 
 def merger_kernel(place_ref, *refs):
-    blocks, tokens, out_ref, weight = refs[:4], refs[4:8], refs[8], refs[9]
+    blocks, nearby, tokens, out_ref, weight = refs[:4], refs[4:6], refs[6:9], refs[9], refs[10]
     for hop in range(4):
         for zh in range(4):
             for k in range(5):
@@ -244,23 +249,25 @@
         for c in range(2):
             total = jnp.zeros((64, 512), F32)
             for zh in range(4):
-                rows = tokens[hop][c, zh * 64 : zh * 64 + 64, :160]
+                span = slice(zh * 64, zh * 64 + 64)
+                rows = nearby[c][span, :160] if hop == 0 else tokens[hop - 1][c, span, :160]
                 total = total + dot(rows, weight[zh * 160 : zh * 160 + 160, :])
             out_ref[place_ref[2 * hop + c]] = total[:, :D_LM].astype(BF)
 
 
-def merger(place, blocks, tokens):
+def merger(place, blocks, nearby, tokens):
     return pl.pallas_call(
         merger_kernel,
         out_shape=jax.ShapeDtypeStruct((8, 64, D_LM), BF),
-        in_specs=[pl.BlockSpec(memory_space=pltpu.SMEM)] + [VMEM] * 8,
+        in_specs=[pl.BlockSpec(memory_space=pltpu.SMEM)] + [VMEM] * 9,
         out_specs=VMEM,
         scratch_shapes=[pltpu.VMEM((640, 512), BF)],
         cost_estimate=pl.CostEstimate(
             flops=340_000_000, bytes_accessed=3_000_000, transcendentals=0
         ),
+        compiler_params=pltpu.CompilerParams(vmem_limit_bytes=12 << 20),
         name="merger",
-    )(place, *blocks, *tokens)
+    )(place, *blocks, *nearby, *tokens)
 
 
 def on_device(
@@ -278,18 +285,13 @@
     kept_count,
 ):
     packed = pack(kept_count, up_weight, down_weight.T, vision_weight)
-    packed, filterbank = lax.optimization_barrier((packed, filterbank))
+    packed, filterbank, patches = lax.optimization_barrier((packed, filterbank, patches))
     blocks = lax.all_to_all(packed, "zh", 0, 0)
 
     span = arrival_spans()
     main = (10 * span[:, None] + jnp.arange(8, dtype=jnp.int32)[None, :]).reshape(-1)
     rest = (10 * span[None, :] + 8 + jnp.arange(2, dtype=jnp.int32)[:, None]).reshape(-1)
     order = jnp.concatenate([main, rest])
-    feature = lax.broadcasted_iota(jnp.int32, (D_ENC, D_ENC), 0)
-    pick = (feature == order[None, :]).astype(BF)
-    audio_rows = lax.dot_general(
-        pick, audio_weight, (((0,), (0,)), ((), ())), preferred_element_type=F32
-    ).astype(BF)
     up = [(i, i + 1) for i in range(N_TM - 1)]
     before = lax.ppermute(filterbank[-1:], TM, up)
     after = lax.ppermute(filterbank[:1], TM, [(j, i) for i, j in up])
@@ -310,40 +312,43 @@
     by_quarter = patch_normed.reshape(64, 4, D_ENC).transpose(1, 0, 2).reshape(256, D_ENC)
     slices = dot(by_quarter, pick_patch).astype(BF)
     core_slices = swap_core(slices[:, 1024:])
-    ranks = jnp.arange(MRG_FRAME, dtype=jnp.int32)
-    by_rank = (retention[0][:, None] == ranks[None, :]).astype(BF)
-
     ffn_hops = around(blocks[:, :, :WIDE], Z, NZ)
     tokens = []
-    for hop, step in enumerate((0, 1, 3, 2)):
-        lanes = slice(256 * hop, 256 * hop + 256)
+    for hop, step in enumerate((1, 3, 2)):
+        lanes = slice(256 * hop + 256, 256 * hop + 512)
         pair = jnp.stack([slices[:, lanes], core_slices[:, lanes]])
         back = [(i, (i - step) % NY) for i in range(NY)]
-        tokens.append(pair if hop == 0 else lax.ppermute(pair, "y", back))
+        tokens.append(lax.ppermute(pair, "y", back))
+    steps = jnp.asarray([0, 0, 1, 1, 3, 3, 2, 2], jnp.int32)
+    flips = jnp.asarray([0, 1] * 4, jnp.int32)
+    place = (2 * ((y + steps) % NY) + jnp.where(flips == 1, 1 - c, c)).astype(jnp.int32)
     ffn_z = jnp.concatenate(ffn_hops, axis=1)
+    vis_block, order_row = blocks[:, :, WIDE:], order[None, :]
+    nearby = (slices[:, :256], core_slices[:, :256])
     spread = jnp.broadcast_to(ffn_z[None], (NY,) + ffn_z.shape)
     own = lax.all_to_all(spread, "y", 0, 0).reshape(512, WIDE)
     hidden, pooled_stem, post = make_stem(
-        filterbank, before, after, conv_weight, both_gains, order[None, :]
+        filterbank, before, after, conv_weight, both_gains, order_row
     )
-    steps = jnp.asarray([0, 0, 1, 1, 3, 3, 2, 2], jnp.int32)
-    flips = jnp.asarray([0, 1] * 4, jnp.int32)
-    place = 2 * ((y + steps) % NY) + jnp.where(flips == 1, 1 - c, c)
-    vis_hops = around(blocks[:, :, WIDE:], Z, NZ)
-    partials = merger(place.astype(jnp.int32), vis_hops, tokens)
+    vis_hops = around(vis_block, Z, NZ)
+    partials = merger(place, vis_hops, nearby, tokens)
     partials = lax.all_to_all(partials, ("y", "c"), 0, 0)
-    own, audio_rows, by_rank, hidden = lax.optimization_barrier(
-        (own, audio_rows, by_rank, hidden)
-    )
+    own, hidden = lax.optimization_barrier((own, hidden))
     other = swap_core(own)
     parts, counts = ffn(hidden, own, other)
+    parts, audio_weight = lax.optimization_barrier((parts, audio_weight))
+    feature = lax.broadcasted_iota(jnp.int32, (D_ENC, D_ENC), 0)
+    pick = (feature == order[None, :]).astype(BF)
+    audio_rows = lax.dot_general(
+        pick, audio_weight, (((0,), (0,)), ((), ())), preferred_element_type=F32
+    ).astype(BF)
     parts = lax.all_to_all(parts, "mod", 0, 0)
     me = lax.axis_index(TM).astype(jnp.int32)
     ids = jnp.arange(N_TM, dtype=jnp.int32)
     wide_span = jnp.broadcast_to(span[:, None], (N_TM, 128))
     ours = jnp.stack([me, kept_count[0]])
     send = tail(
-        ours, parts, pooled_stem, post, audio_rows, partials, by_rank, counts, wide_span
+        ours, parts, pooled_stem, post, audio_rows, partials, retention, counts, wide_span
     )
     counts, send = lax.optimization_barrier((counts, send))
     placed = counts[:, 0].astype(jnp.int32) + AUD_TOK

time: 216 us -> 215 us (level)
  waiting for transfers between devices: 73.8 us -> 79.9 us
  Pallas kernels: 18.1 us -> 13.3 us
  starting transfers between devices: 69.4 us -> 65.8 us
    ppermute x1, waiting for transfers between devices: 24.4 us -> 30 us  [on_device(): before = lax.ppermute(filterbank[-1:], TM, up)]
    ppermute x6, waiting for transfers between devices: 16.6 us -> 20.9 us  [around(): lax.ppermute(value, axis, [(i, (i + shift) % size) for i in range(size)])]
    all_to_all x1, waiting for transfers between devices: 9.16 us -> 5.2 us  [on_device(): parts = lax.all_to_all(parts, 'mod', 0, 0)]
    all_to_all x1, starting transfers between devices: 8.07 us -> 4.45 us  [on_device(): partials = lax.all_to_all(partials, ('y', 'c'), 0, 0)]
  transfers between devices with their start and end apart: 17 -> 17, of which waited for: 9 -> 10; matrix products, arithmetic and copies ran while one was open for 5% -> 6% of each run, Pallas kernels for 6% -> 5%
where the time goes in v1:
time: 215 us; the launch traced here: 214 us
  waiting for transfers between devices  79.9 us (37%)
  starting transfers between devices  65.8 us (31%)
  blocking collectives  33.2 us (15%)
  Pallas kernels  13.3 us (6%)
  local copies, waits for them, and re-layouts  9.72 us (5%)
  matrix products  7.03 us (3%)
  other arithmetic  3.94 us (2%)
    all_to_all x1, blocking collectives, on_device(): blocks = lax.all_to_all(packed, 'zh', 0, 0)  33.2 us
    ppermute x1, waiting for transfers between devices, on_device(): before = lax.ppermute(filterbank[-1:], TM, up)  30 us
    ppermute x6, starting transfers between devices, around(): lax.ppermute(value, axis, [(i, (i + shift) % size) for i in range(size)])  25.5 us
    ppermute x6, waiting for transfers between devices, around(): lax.ppermute(value, axis, [(i, (i + shift) % size) for i in range(size)])  20.9 us
    all_to_all x1, waiting for transfers between devices, on_device(): lax.all_to_all(send.reshape(N_TM, 1, D_LM), TM, 0, 0).reshape(N_TM, D_LM)  15.9 us
    ppermute x3, starting transfers between devices, on_device(): tokens.append(lax.ppermute(pair, 'y', back))  9.27 us
    all_to_all x1, starting transfers between devices, on_device(): lax.all_to_all(send.reshape(N_TM, 1, D_LM), TM, 0, 0).reshape(N_TM, D_LM)  7.26 us
    pallas_call x1, Pallas kernels, ffn(): pl.pallas_call(ffn_kernel, out_shape=(jax.ShapeDtypeStruct((NM, 64, D_ENC...  5.96 us
  transfers between devices with their start and end apart: 17, of which 10 were waited for; matrix products, arithmetic and copies ran while one was open for 6% of the time, Pallas kernels for 5%

profile of v1, /device:TPU:1, one launch (start us, length us, event | category | flops | bytes accessed | tf_op | source)
XLA Modules:
  0.0 214.1 jit_solution(11729799584946580425)
XLA Ops:
  0.7 1.6 pack.1
  2.3 33.2 %all_to_all.25 = bf16[4,8,5888]{2,1,0:T(8,128)(2,1)S(1)} all-to-all(bf16[4,8,5888]{2,1,0:T(8,128)(2,1)} %pack.1), channel_id=1, replica_groups=mesh['zh'=4,'zl'=4,'y'=4,'c'=2,'mod'=4] {'zh'}, dimensions={0} | all-to-all | bytes 753664 | tf_op jit(solution)/shard_map/all_to_all | solution.py:289
  35.5 11.4 %collective-permute-start.2 = (bf16[4,8,3328]{2,1,0:T(8,128)(2,1)S(1)}, bf16[4,8,3328]{2,1,0:T(8,128)(2,1)S(1)}, u32[]{:S(2)}, u32[]{:S(2)}) collective-permute-start(bf16[4,8,3328]{2,1,0:T(8,128)(2,1)S(1)} %slice.56), channel_id=1, source_target_pairs={{0,64},{32,96},{64,128},{96,160},{128,192},{160,224},{192,256},{22... | collective-permute-start | bytes 638984 | tf_op jit(solution)/shard_map/ppermute | solution.py:40
  46.9 3.8 %collective-permute-start.1 = (bf16[4,8,3328]{2,1,0:T(8,128)(2,1)S(1)}, bf16[4,8,3328]{2,1,0:T(8,128)(2,1)S(1)}, u32[]{:S(2)}, u32[]{:S(2)}) collective-permute-start(bf16[4,8,3328]{2,1,0:T(8,128)(2,1)S(1)} %slice.56), channel_id=1, source_target_pairs={{0,480},{32,0},{64,32},{96,64},{128,96},{160,128},{192,160},{224,1... | collective-permute-start | bytes 638984 | tf_op jit(solution)/shard_map/ppermute | solution.py:40
  50.7 1.9 collective-permute-start
  52.6 4.0 %collective-permute-done.2 = bf16[4,8,3328]{2,1,0:T(8,128)(2,1)S(1)} collective-permute-done((bf16[4,8,3328]{2,1,0:T(8,128)(2,1)S(1)}, bf16[4,8,3328]{2,1,0:T(8,128)(2,1)S(1)}, u32[]{:S(2)}, u32[]{:S(2)}) %collective-permute-start.2) | collective-permute-done | bytes 213024 | tf_op jit(solution)/shard_map/ppermute | solution.py:40
  56.6 6.4 %collective-permute-done = bf16[4,8,3328]{2,1,0:T(8,128)(2,1)S(1)} collective-permute-done((bf16[4,8,3328]{2,1,0:T(8,128)(2,1)S(1)}, bf16[4,8,3328]{2,1,0:T(8,128)(2,1)S(1)}, u32[]{:S(2)}, u32[]{:S(2)}) %collective-permute-start) | collective-permute-done | bytes 213024 | tf_op jit(solution)/shard_map/ppermute | solution.py:40
  63.1 2.1 broadcast_in_dim.90
  65.2 4.9 %all-to-all-start.1 = ((bf16[4,4,32,3328]{3,2,1,0:T(8,128)(2,1)}), bf16[4,4,32,3328]{3,2,1,0:T(8,128)(2,1)}, u32[]{:S(2)}, u32[]{:S(2)}) async-start(bf16[4,4,32,3328]{3,2,1,0:T(8,128)(2,1)} %broadcast_in_dim.90), calls=%async_computation.1 | async-start | bytes 6815744 | tf_op jit(solution)/shard_map/all_to_all | solution.py:329
  70.1 4.2 %collective-permute-start.3 = (bf16[1,128]{1,0:T(2,128)(2,1)S(1)}, bf16[1,128]{1,0:T(2,128)(2,1)S(1)}, u32[]{:S(2)}, u32[]{:S(2)}) collective-permute-start(bf16[1,128]{1,0:T(2,128)(2,1)S(1)} %get-tuple-element.46), channel_id=1, source_target_pairs={{0,4},{4,8},{8,12},{12,16},{16,20},{20,24},{24,28},{28,32},{32,36}... | collective-permute-start | bytes 776 | tf_op jit(solution)/shard_map/ppermute | solution.py:296
  74.3 1.9 collective-permute-start.4
  76.5 30.0 %collective-permute-done.3.before_ref = bf16[1,128]{1,0:T(2,128)(2,1)S(1)} collective-permute-done((bf16[1,128]{1,0:T(2,128)(2,1)S(1)}, bf16[1,128]{1,0:T(2,128)(2,1)S(1)}, u32[]{:S(2)}, u32[]{:S(2)}) %collective-permute-start.3) | collective-permute-done | bytes 288 | tf_op jit(solution)/shard_map/ppermute | solution.py:296
  106.5 3.0 %collective-permute-done.4.after_ref = bf16[1,128]{1,0:T(2,128)(2,1)S(1)} collective-permute-done((bf16[1,128]{1,0:T(2,128)(2,1)S(1)}, bf16[1,128]{1,0:T(2,128)(2,1)S(1)}, u32[]{:S(2)}, u32[]{:S(2)}) %collective-permute-start.4) | collective-permute-done | bytes 288 | tf_op jit(solution)/shard_map/ppermute | solution.py:297
  109.6 2.2 %stem.1 = (bf16[128,1280]{1,0:T(8,128)(2,1)S(1)}, f32[64,1280]{1,0:T(8,128)S(1)}, f32[1,1280]{1,0:T(1,128)S(1)}) custom-call(bf16[128,128]{1,0:T(8,128)(2,1)S(1)} %copy-done.6, bf16[1,128]{1,0:T(2,128)(2,1)S(1)} %collective-permute-done.3.before_ref, bf16[1,128]{1,0:T(2,128)(2,1)S(1)} %collective-permute-done.4.after_ref, bf16[384,1280]{1,0:T(8,128)(2,1)S(1)} %copy-done.7, ...), custom_call_target="tpu_custom_call" | custom-call | flops 1500000000 | bytes 2500000 | tf_op jit(solution)/shard_map/stem/pallas_call | solution.py:133
  111.8 1.9 collective-permute-start.5
  113.7 1.3 fusion.6
  115.1 1.3 fusion.8
  116.5 0.9 copy.30
  117.4 3.3 %fusion.5 = bf16[256,2048]{1,0:T(8,128)(2,1)S(1)} fusion(bf16[256,1280]{1,0:T(8,128)(2,1)} %bitcast.29, s32[2048]{0:T(1024)S(1)} %fusion.18), kind=kOutput, calls=%fused_computation.7 | convolution fusion | flops 1345323008 | bytes 1712128 | tf_op jit(solution)/shard_map/dot_general | solution.py:62
  120.8 2.4 %collective-permute-start.9 = (bf16[256,1024]{1,0:T(8,128)(2,1)S(1)}, bf16[256,1024]{1,0:T(8,128)(2,1)S(1)}, u32[]{:S(2)}, u32[]{:S(2)}) collective-permute-start(bf16[256,1024]{1,0:T(8,128)(2,1)S(1)} %slice.59), channel_id=1, source_target_pairs={{0,4},{4,0},{1,5},{5,1},{2,6},{6,2},{3,7},{7,3},{8,12},{12,8},{9,1... | collective-permute-start | bytes 1572872 | tf_op jit(solution)/shard_map/ppermute | solution.py:46
  123.3 1.4 collective-permute-done.9
  124.8 2.7 %collective-permute-start.10 = (bf16[2,256,256]{2,1,0:T(8,128)(2,1)S(1)}, bf16[2,256,256]{2,1,0:T(8,128)(2,1)S(1)}, u32[]{:S(2)}, u32[]{:S(2)}) collective-permute-start(bf16[2,256,256]{2,1,0:T(8,128)(2,1)S(1)} %pad_maximum_fusion.1), channel_id=1, source_target_pairs={{0,24},{8,0},{16,8},{24,16},{1,25},{9,1},{17,9},{25,17},{2,26},{10... | collective-permute-start | bytes 786440 | tf_op jit(solution)/shard_map/ppermute | solution.py:321
  127.6 2.5 %collective-permute-start.11 = (bf16[2,256,256]{2,1,0:T(8,128)(2,1)S(1)}, bf16[2,256,256]{2,1,0:T(8,128)(2,1)S(1)}, u32[]{:S(2)}, u32[]{:S(2)}) collective-permute-start(bf16[2,256,256]{2,1,0:T(8,128)(2,1)S(1)} %pad_maximum_fusion.2), channel_id=1, source_target_pairs={{0,8},{8,16},{16,24},{24,0},{1,9},{9,17},{17,25},{25,1},{2,10},{10... | collective-permute-start | bytes 786440 | tf_op jit(solution)/shard_map/ppermute | solution.py:321
  130.2 4.0 %collective-permute-start.12 = (bf16[2,256,256]{2,1,0:T(8,128)(2,1)S(1)}, bf16[2,256,256]{2,1,0:T(8,128)(2,1)S(1)}, u32[]{:S(2)}, u32[]{:S(2)}) collective-permute-start(bf16[2,256,256]{2,1,0:T(8,128)(2,1)S(1)} %pad_maximum_fusion.3), channel_id=1, source_target_pairs={{0,16},{8,24},{16,0},{24,8},{1,17},{9,25},{17,1},{25,9},{2,18},{10... | collective-permute-start | bytes 786440 | tf_op jit(solution)/shard_map/ppermute | solution.py:321
  134.2 0.9 slice.57.refs_0_
  135.1 1.9 collective-permute-start.6
  137.1 4.6 %collective-permute-start.7 = (bf16[4,8,2560]{2,1,0:T(8,128)(2,1)S(1)}, bf16[4,8,2560]{2,1,0:T(8,128)(2,1)S(1)}, u32[]{:S(2)}, u32[]{:S(2)}) collective-permute-start(bf16[4,8,2560]{2,1,0:T(8,128)(2,1)S(1)} %slice.57.refs_0_), channel_id=1, source_target_pairs={{0,480},{32,0},{64,32},{96,64},{128,96},{160,128},{192,160},{224,1... | collective-permute-start | bytes 491528 | tf_op jit(solution)/shard_map/ppermute | solution.py:40
  141.6 1.9 collective-permute-start.8
  143.6 0.2 collective-permute-done.7.refs_2_
  143.9 10.3 %collective-permute-done.8.refs_3_ = bf16[4,8,2560]{2,1,0:T(8,128)(2,1)S(1)} collective-permute-done((bf16[4,8,2560]{2,1,0:T(8,128)(2,1)S(1)}, bf16[4,8,2560]{2,1,0:T(8,128)(2,1)S(1)}, u32[]{:S(2)}, u32[]{:S(2)}) %collective-permute-start.8) | collective-permute-done | bytes 163872 | tf_op jit(solution)/shard_map/ppermute | solution.py:40
  154.2 2.2 %merger.1 = bf16[8,64,448]{2,1,0:T(8,128)(2,1)} custom-call(s32[8]{0:T(128)S(1)} %fusion.41.place_ref, bf16[4,8,2560]{2,1,0:T(8,128)(2,1)S(1)} %slice.57.refs_0_, bf16[4,8,2560]{2,1,0:T(8,128)(2,1)S(1)} %collective-permute-done.6.refs_1_, bf16[4,8,2560]{2,1,0:T(8,128)(2,1)S(1)} %collective-permute-done.7.refs_2_, ...), custom_call_target="tpu_custom_call" | custom-call | flops 340000000 | bytes 3000000 | tf_op jit(solution)/shard_map/merger/pallas_call | solution.py:259
  156.4 4.4 %all-to-all-start.3 = ((bf16[8,64,448]{2,1,0:T(8,128)(2,1)}), bf16[8,64,448]{2,1,0:T(8,128)(2,1)S(1)}, u32[]{:S(2)}, u32[]{:S(2)}) async-start(bf16[8,64,448]{2,1,0:T(8,128)(2,1)} %merger.1), calls=%async_computation.3 | async-start | bytes 1048576 | tf_op jit(solution)/shard_map/all_to_all | solution.py:335
  160.8 6.0 %ffn.1 = (bf16[4,64,1280]{2,1,0:T(8,128)(2,1)}, f32[128,128]{1,0:T(8,128)S(1)}) custom-call(bf16[128,1280]{1,0:T(8,128)(2,1)S(1)} %get-tuple-element.22.hidden_ref, bf16[512,3328]{1,0:T(8,128)(2,1)} %bitcast.1.own_ref, bf16[512,3328]{1,0:T(8,128)(2,1)} %collective-permute-done.5.other_ref), custom_call_target="tpu_custom_call" | custom-call | flops 650000000 | bytes 8000000 | tf_op jit(solution)/shard_map/ffn/pallas_call | solution.py:179
  166.8 3.4 %all-to-all-done.3.vis_ref = bf16[8,64,448]{2,1,0:T(8,128)(2,1)S(1)} async-done(((bf16[8,64,448]{2,1,0:T(8,128)(2,1)}), bf16[8,64,448]{2,1,0:T(8,128)(2,1)S(1)}, u32[]{:S(2)}, u32[]{:S(2)}) %all-to-all-start.3) | async-done | bytes 458784 | tf_op jit(solution)/shard_map/all_to_all | solution.py:335
  170.2 4.0 %all-to-all-start.2 = ((bf16[4,64,1280]{2,1,0:T(8,128)(2,1)}), bf16[4,64,1280]{2,1,0:T(8,128)(2,1)S(1)}, u32[]{:S(2)}, u32[]{:S(2)}) async-start(bf16[4,64,1280]{2,1,0:T(8,128)(2,1)} %get-tuple-element.26), calls=%async_computation.2 | async-start | bytes 1310720 | tf_op jit(solution)/shard_map/all_to_all | solution.py:345
  174.3 2.9 %fusion.4 = bf16[1280,448]{0,1:T(8,128)(2,1)} fusion(bf16[1280,448]{0,1:T(8,128)(2,1)S(1)} %copy-done, s32[1280]{0:T(1024)S(1)} %pad_add_fusion), kind=kOutput, calls=%fused_computation.6 | convolution fusion | flops 1470218240 | bytes 2298880 | tf_op jit(solution)/shard_map/dot_general | solution.py:342
  177.2 1.6 copy.31.audio_ref
  178.8 5.2 %all-to-all-done.2.part_ref = bf16[4,64,1280]{2,1,0:T(8,128)(2,1)S(1)} async-done(((bf16[4,64,1280]{2,1,0:T(8,128)(2,1)}), bf16[4,64,1280]{2,1,0:T(8,128)(2,1)S(1)}, u32[]{:S(2)}, u32[]{:S(2)}) %all-to-all-start.2) | async-done | bytes 655392 | tf_op jit(solution)/shard_map/all_to_all | solution.py:345
  184.1 1.0 copy-done.2
  185.1 1.0 copy-done.4
  186.1 1.3 tail.1
  187.4 0.6 broadcast.966
  188.0 0.7 reduce.2
  188.7 0.8 reshape.326
  189.5 7.3 %all-to-all-start.4 = ((bf16[128,2,224]{2,1,0:T(2,128)(2,1)}), bf16[128,2,224]{2,1,0:T(2,128)(2,1)S(1)}, u32[]{:S(2)}, u32[]{:S(2)}) async-start(bf16[128,2,224]{2,1,0:T(2,128)(2,1)} %reshape.326), calls=%async_computation.4 | async-start | bytes 262144 | tf_op jit(solution)/shard_map/all_to_all | solution.py:357
  197.0 15.9 %all-to-all-done.4 = bf16[128,2,224]{2,1,0:T(2,128)(2,1)S(1)} async-done(((bf16[128,2,224]{2,1,0:T(2,128)(2,1)}), bf16[128,2,224]{2,1,0:T(2,128)(2,1)S(1)}, u32[]{:S(2)}, u32[]{:S(2)}) %all-to-all-start.4) | async-done | bytes 114720 | tf_op jit(solution)/shard_map/all_to_all | solution.py:357
  213.0 0.2 copy.33
  213.2 0.8 fusion.9
  (62 shorter events, 1.3 us)
Async XLA Ops:
  0.0 174.3 %copy-start = (bf16[1280,448]{0,1:T(8,128)(2,1)S(1)}, bf16[1280,448]{0,1:T(8,128)(2,1)}, u32[]{:S(2)}) copy-start(bf16[1280,448]{0,1:T(8,128)(2,1)} %param.20) | copy-start | bytes 3440644
  35.5 21.1 %copy-start.8 = (bf16[4,8,5888]{2,1,0:T(8,128)(2,1)}, bf16[4,8,5888]{2,1,0:T(8,128)(2,1)S(1)}, u32[]{:S(2)}) copy-start(bf16[4,8,5888]{2,1,0:T(8,128)(2,1)S(1)} %all_to_all.25) | copy-start | bytes 1130500
  35.5 21.1 %collective-permute-start.2 = (bf16[4,8,3328]{2,1,0:T(8,128)(2,1)S(1)}, bf16[4,8,3328]{2,1,0:T(8,128)(2,1)S(1)}, u32[]{:S(2)}, u32[]{:S(2)}) collective-permute-start(bf16[4,8,3328]{2,1,0:T(8,128)(2,1)S(1)} %slice.56), channel_id=1, source_target_pairs={{0,64},{32,96},{64,128},{96,160},{128,192},{160,224},{192,256},{22... | collective-permute-start | bytes 638984 | tf_op jit(solution)/shard_map/ppermute | solution.py:40
  46.9 9.7 %collective-permute-start.1 = (bf16[4,8,3328]{2,1,0:T(8,128)(2,1)S(1)}, bf16[4,8,3328]{2,1,0:T(8,128)(2,1)S(1)}, u32[]{:S(2)}, u32[]{:S(2)}) collective-permute-start(bf16[4,8,3328]{2,1,0:T(8,128)(2,1)S(1)} %slice.56), channel_id=1, source_target_pairs={{0,480},{32,0},{64,32},{96,64},{128,96},{160,128},{192,160},{224,1... | collective-permute-start | bytes 638984 | tf_op jit(solution)/shard_map/ppermute | solution.py:40
  50.7 12.3 %collective-permute-start = (bf16[4,8,3328]{2,1,0:T(8,128)(2,1)S(1)}, bf16[4,8,3328]{2,1,0:T(8,128)(2,1)S(1)}, u32[]{:S(2)}, u32[]{:S(2)}) collective-permute-start(bf16[4,8,3328]{2,1,0:T(8,128)(2,1)S(1)} %slice.56), channel_id=1, source_target_pairs={{0,32},{32,64},{64,96},{96,128},{128,160},{160,192},{192,224},{224... | collective-permute-start | bytes 638984 | tf_op jit(solution)/shard_map/ppermute | solution.py:40
  65.2 4.9 %copy-start.6 = (bf16[128,128]{1,0:T(8,128)(2,1)S(1)}, bf16[128,128]{1,0:T(8,128)(2,1)}, u32[]{:S(2)}) copy-start(bf16[128,128]{1,0:T(8,128)(2,1)} %frames_ref) | copy-start | bytes 98308
  65.2 11.0 %copy-start.10 = (f32[1280]{0:T(1024)S(1)}, f32[1280]{0:T(1024)}, u32[]{:S(2)}) copy-start(f32[1280]{0:T(1024)} %param.19) | copy-start | bytes 15364
  65.2 11.0 %copy-start.11 = (f32[1280]{0:T(1024)S(1)}, f32[1280]{0:T(1024)}, u32[]{:S(2)}) copy-start(f32[1280]{0:T(1024)} %param.16) | copy-start | bytes 15364
  65.2 44.4 %copy-start.7 = (bf16[384,1280]{1,0:T(8,128)(2,1)S(1)}, bf16[384,1280]{1,0:T(8,128)(2,1)}, u32[]{:S(2)}) copy-start(bf16[384,1280]{1,0:T(8,128)(2,1)} %conv_ref.1) | copy-start | bytes 2949124
  65.2 46.6 %all-to-all-start.1 = ((bf16[4,4,32,3328]{3,2,1,0:T(8,128)(2,1)}), bf16[4,4,32,3328]{3,2,1,0:T(8,128)(2,1)}, u32[]{:S(2)}, u32[]{:S(2)}) async-start(bf16[4,4,32,3328]{3,2,1,0:T(8,128)(2,1)} %broadcast_in_dim.90), calls=%async_computation.1 | async-start | bytes 6815744 | tf_op jit(solution)/shard_map/all_to_all | solution.py:329
  70.1 36.4 %collective-permute-start.3 = (bf16[1,128]{1,0:T(2,128)(2,1)S(1)}, bf16[1,128]{1,0:T(2,128)(2,1)S(1)}, u32[]{:S(2)}, u32[]{:S(2)}) collective-permute-start(bf16[1,128]{1,0:T(2,128)(2,1)S(1)} %get-tuple-element.46), channel_id=1, source_target_pairs={{0,4},{4,8},{8,12},{12,16},{16,20},{20,24},{24,28},{28,32},{32,36}... | collective-permute-start | bytes 776 | tf_op jit(solution)/shard_map/ppermute | solution.py:296
  74.3 35.3 %collective-permute-start.4 = (bf16[1,128]{1,0:T(2,128)(2,1)S(1)}, bf16[1,128]{1,0:T(2,128)(2,1)S(1)}, u32[]{:S(2)}, u32[]{:S(2)}) collective-permute-start(bf16[1,128]{1,0:T(2,128)(2,1)S(1)} %get-tuple-element.45), channel_id=1, source_target_pairs={{4,0},{8,4},{12,8},{16,12},{20,16},{24,20},{28,24},{32,28},{36,32}... | collective-permute-start | bytes 776 | tf_op jit(solution)/shard_map/ppermute | solution.py:297
  76.5 38.5 %copy-start.9 = (f32[1280]{0:T(1024)S(1)}, f32[1280]{0:T(1024)}, u32[]{:S(2)}) copy-start(f32[1280]{0:T(1024)} %param.22) | copy-start | bytes 15364
  111.8 5.6 %copy-start.3 = (f32[64,1280]{1,0:T(8,128)}, f32[64,1280]{1,0:T(8,128)S(1)}, u32[]{:S(2)}) copy-start(f32[64,1280]{1,0:T(8,128)S(1)} %get-tuple-element.27.stem_ref) | copy-start | bytes 983044
  111.8 49.0 %collective-permute-start.5 = (bf16[512,3328]{1,0:T(8,128)(2,1)}, bf16[512,3328]{1,0:T(8,128)(2,1)}, u32[]{:S(2)}, u32[]{:S(2)}) collective-permute-start(bf16[512,3328]{1,0:T(8,128)(2,1)} %bitcast.1.own_ref), channel_id=1, source_target_pairs={{0,4},{4,0},{1,5},{5,1},{2,6},{6,2},{3,7},{7,3},{8,12},{12,8},{9,1... | collective-permute-start | bytes 10223624 | tf_op jit(solution)/shard_map/ppermute | solution.py:46
  120.8 3.9 %collective-permute-start.9 = (bf16[256,1024]{1,0:T(8,128)(2,1)S(1)}, bf16[256,1024]{1,0:T(8,128)(2,1)S(1)}, u32[]{:S(2)}, u32[]{:S(2)}) collective-permute-start(bf16[256,1024]{1,0:T(8,128)(2,1)S(1)} %slice.59), channel_id=1, source_target_pairs={{0,4},{4,0},{1,5},{5,1},{2,6},{6,2},{3,7},{7,3},{8,12},{12,8},{9,1... | collective-permute-start | bytes 1572872 | tf_op jit(solution)/shard_map/ppermute | solution.py:46
  123.3 20.3 %copy-start.12 = (s32[8]{0:T(128)S(1)}, s32[8]{0:T(128)}, u32[]{:S(2)}) copy-start(s32[8]{0:T(128)} %constant.219.clone) | copy-start | bytes 100
  123.3 20.3 %copy-start.13 = (pred[8]{0:T(512)(128)(4,1)S(1)}, pred[8]{0:T(512)(128)(4,1)}, u32[]{:S(2)}) copy-start(pred[8]{0:T(512)(128)(4,1)} %constant.228) | copy-start | bytes 28
  124.8 12.2 %collective-permute-start.10 = (bf16[2,256,256]{2,1,0:T(8,128)(2,1)S(1)}, bf16[2,256,256]{2,1,0:T(8,128)(2,1)S(1)}, u32[]{:S(2)}, u32[]{:S(2)}) collective-permute-start(bf16[2,256,256]{2,1,0:T(8,128)(2,1)S(1)} %pad_maximum_fusion.1), channel_id=1, source_target_pairs={{0,24},{8,0},{16,8},{24,16},{1,25},{9,1},{17,9},{25,17},{2,26},{10... | collective-permute-start | bytes 786440 | tf_op jit(solution)/shard_map/ppermute | solution.py:321
  127.6 14.0 %collective-permute-start.11 = (bf16[2,256,256]{2,1,0:T(8,128)(2,1)S(1)}, bf16[2,256,256]{2,1,0:T(8,128)(2,1)S(1)}, u32[]{:S(2)}, u32[]{:S(2)}) collective-permute-start(bf16[2,256,256]{2,1,0:T(8,128)(2,1)S(1)} %pad_maximum_fusion.2), channel_id=1, source_target_pairs={{0,8},{8,16},{16,24},{24,0},{1,9},{9,17},{17,25},{25,1},{2,10},{10... | collective-permute-start | bytes 786440 | tf_op jit(solution)/shard_map/ppermute | solution.py:321
  130.2 13.4 %collective-permute-start.12 = (bf16[2,256,256]{2,1,0:T(8,128)(2,1)S(1)}, bf16[2,256,256]{2,1,0:T(8,128)(2,1)S(1)}, u32[]{:S(2)}, u32[]{:S(2)}) collective-permute-start(bf16[2,256,256]{2,1,0:T(8,128)(2,1)S(1)} %pad_maximum_fusion.3), channel_id=1, source_target_pairs={{0,16},{8,24},{16,0},{24,8},{1,17},{9,25},{17,1},{25,9},{2,18},{10... | collective-permute-start | bytes 786440 | tf_op jit(solution)/shard_map/ppermute | solution.py:321
  135.1 8.5 %collective-permute-start.6 = (bf16[4,8,2560]{2,1,0:T(8,128)(2,1)S(1)}, bf16[4,8,2560]{2,1,0:T(8,128)(2,1)S(1)}, u32[]{:S(2)}, u32[]{:S(2)}) collective-permute-start(bf16[4,8,2560]{2,1,0:T(8,128)(2,1)S(1)} %slice.57.refs_0_), channel_id=1, source_target_pairs={{0,32},{32,64},{64,96},{96,128},{128,160},{160,192},{192,224},{224... | collective-permute-start | bytes 491528 | tf_op jit(solution)/shard_map/ppermute | solution.py:40
  137.1 6.8 %collective-permute-start.7 = (bf16[4,8,2560]{2,1,0:T(8,128)(2,1)S(1)}, bf16[4,8,2560]{2,1,0:T(8,128)(2,1)S(1)}, u32[]{:S(2)}, u32[]{:S(2)}) collective-permute-start(bf16[4,8,2560]{2,1,0:T(8,128)(2,1)S(1)} %slice.57.refs_0_), channel_id=1, source_target_pairs={{0,480},{32,0},{64,32},{96,64},{128,96},{160,128},{192,160},{224,1... | collective-permute-start | bytes 491528 | tf_op jit(solution)/shard_map/ppermute | solution.py:40
  141.6 12.5 %collective-permute-start.8 = (bf16[4,8,2560]{2,1,0:T(8,128)(2,1)S(1)}, bf16[4,8,2560]{2,1,0:T(8,128)(2,1)S(1)}, u32[]{:S(2)}, u32[]{:S(2)}) collective-permute-start(bf16[4,8,2560]{2,1,0:T(8,128)(2,1)S(1)} %slice.57.refs_0_), channel_id=1, source_target_pairs={{0,64},{32,96},{64,128},{96,160},{128,192},{160,224},{192,256},{22... | collective-permute-start | bytes 491528 | tf_op jit(solution)/shard_map/ppermute | solution.py:40
  156.4 13.8 %all-to-all-start.3 = ((bf16[8,64,448]{2,1,0:T(8,128)(2,1)}), bf16[8,64,448]{2,1,0:T(8,128)(2,1)S(1)}, u32[]{:S(2)}, u32[]{:S(2)}) async-start(bf16[8,64,448]{2,1,0:T(8,128)(2,1)} %merger.1), calls=%async_computation.3 | async-start | bytes 1048576 | tf_op jit(solution)/shard_map/all_to_all | solution.py:335
  170.2 4.1 %copy-start.1 = (bf16[8,64,448]{2,1,0:T(8,128)(2,1)}, bf16[8,64,448]{2,1,0:T(8,128)(2,1)S(1)}, u32[]{:S(2)}) copy-start(bf16[8,64,448]{2,1,0:T(8,128)(2,1)S(1)} %all-to-all-done.3.vis_ref) | copy-start | bytes 1376260
  170.2 13.8 %all-to-all-start.2 = ((bf16[4,64,1280]{2,1,0:T(8,128)(2,1)}), bf16[4,64,1280]{2,1,0:T(8,128)(2,1)S(1)}, u32[]{:S(2)}, u32[]{:S(2)}) async-start(bf16[4,64,1280]{2,1,0:T(8,128)(2,1)} %get-tuple-element.26), calls=%async_computation.2 | async-start | bytes 1310720 | tf_op jit(solution)/shard_map/all_to_all | solution.py:345
  177.2 6.9 %copy-start.5 = (s32[1,64]{1,0:T(1,128)S(1)}, s32[1,64]{1,0:T(1,128)}, u32[]{:S(2)}) copy-start(s32[1,64]{1,0:T(1,128)} %rank_ref.1) | copy-start | bytes 772
  184.1 1.0 copy-start.2
  185.1 1.0 copy-start.4
  189.5 23.4 %all-to-all-start.4 = ((bf16[128,2,224]{2,1,0:T(2,128)(2,1)}), bf16[128,2,224]{2,1,0:T(2,128)(2,1)S(1)}, u32[]{:S(2)}, u32[]{:S(2)}) async-start(bf16[128,2,224]{2,1,0:T(2,128)(2,1)} %reshape.326), calls=%async_computation.4 | async-start | bytes 262144 | tf_op jit(solution)/shard_map/all_to_all | solution.py:357
